TPU v7x, 128 devices: a whole 4x4x4 slice. The times are simulated.
128 devices in a mesh: pb: 4 (over z_hi, core), ka: 32 (over z_lo, y, x).
Axes of the slice: x: 4, y: 4, z: 4 (z_hi: 2, z_lo: 2; z = z_hi * 2 + z_lo), core: 2. Of those that a mesh axis runs over, the one named last changes fastest.
Arguments:
- vertex_ladder: float32 [2, 16, 1024, 1024], P(None, 'pb', 'ka'), may hold values from -6 to 6
- vertex_cross_a: float32 [2, 16, 1024, 1024], P(None, 'pb', 'ka'), may hold values from -6 to 6
- vertex_cross_b: float32 [2, 16, 1024, 1024], P(None, 'pb', 'ka'), may hold values from -6 to 6
- bubble: float32 [2, 16, 1024], P(None, 'pb'), may hold values from -0.072 to 0.072
- row_maps: int32 [2, 16, 1024], replicated, may hold values from 0 to 16383, as said below
- col_maps: int32 [2, 1024], replicated, may hold values from 0 to 1023, each once within a row
Outputs:
- ladder_out: float32 [2, 16, 1024, 1024], P(None, 'pb', 'ka')
- crossed_a: float32 [2, 16, 1024, 1024], P(None, 'pb', 'ka')
- crossed_b: float32 [2, 16, 1024, 1024], P(None, 'pb', 'ka')
Inputs may be any that keep to these rules, and one draw needn't show every extreme that they name: `row_maps`: each of the two maps is a permutation of all 16384 rows. A device holds the rows of its bosonic indices (index of pb) and its first fermionic indices (index of ka); the 128 rows of one device take exactly 1 of their source rows from each device.
All inputs are finite; a program needn't handle non-finite values.
Results may differ from a plain program's by a relative error of at most 0.007.
Values may be sent and summed in bfloat16 or wider, within the bound.
A program may use at most 64 MiB of HBM per device.

v0:
```python
import jax
import jax.numpy as jnp
from jax import lax
from jax.sharding import PartitionSpec as P

LADDER = 6


def in_one_piece(arrays, axis, split_dim, concat_dim, along):
    ends, at = ([], 0)
    for a in arrays[:-1]:
        at += a.shape[along]
        ends.append(at)
    both = jnp.concatenate(arrays, axis=along)
    return tuple(
        jnp.split(
            lax.all_to_all(both, axis, split_axis=split_dim, concat_axis=concat_dim, tiled=True),
            ends,
            axis=along,
        )
    )


def ladder_rows(vertex_rows, bubble_q, gathered):
    col_count = gathered.shape[2]
    row_count = vertex_rows.shape[1]
    right_op = jnp.concatenate([gathered[0], gathered[1]], 1)
    current = vertex_rows
    for _ in range(LADDER):
        scaled_re = current[0] * bubble_q[0][None, :] - current[1] * bubble_q[1][None, :]
        scaled_im = current[0] * bubble_q[1][None, :] + current[1] * bubble_q[0][None, :]
        left_op = jnp.concatenate([scaled_re, scaled_im], 0).astype(jnp.bfloat16)
        product = jnp.dot(left_op, right_op, preferred_element_type=jnp.float32)
        real_part = product[:row_count, :col_count] - product[row_count:, col_count:]
        imag_part = product[:row_count, col_count:] + product[row_count:, :col_count]
        current = vertex_rows + jnp.stack([real_part, imag_part])
    return current


def per_device(vertex_ladder, vertex_cross_a, vertex_cross_b, bubble, row_maps, col_maps):
    q_local = vertex_ladder.shape[1]
    row_count = vertex_ladder.shape[2]
    col_count = vertex_ladder.shape[3]
    gamma_low = vertex_ladder.astype(jnp.bfloat16)
    whole_low = lax.all_gather(gamma_low, "ka", axis=2, tiled=True)

    def per_whole(loop_state, scan_items):
        vertex_rows, gathered, bubble_q = scan_items
        return (loop_state, ladder_rows(vertex_rows, bubble_q, gathered))

    _, stacked = lax.scan(
        per_whole,
        jnp.int32(0),
        (
            jnp.moveaxis(vertex_ladder, 1, 0),
            jnp.moveaxis(whole_low, 1, 0),
            jnp.moveaxis(bubble, 1, 0),
        ),
    )
    ladder_out = jnp.moveaxis(stacked, 0, 1)
    local_count = q_local * row_count
    reducible = (ladder_out - vertex_ladder).reshape(2, local_count, col_count)
    pb_count = lax.axis_size("pb")
    ka_count = lax.axis_size("ka")
    dev_count = pb_count * ka_count
    per_peer = local_count // dev_count
    my_device = lax.axis_index("pb") * ka_count + lax.axis_index("ka")
    my_bos = lax.axis_index("pb") * q_local + jnp.arange(q_local, dtype=jnp.int32)
    my_fer = lax.axis_index("ka") * row_count + jnp.arange(row_count, dtype=jnp.int32)
    my_rows = (my_bos[:, None] * col_count + my_fer[None, :]).reshape(-1)
    slot_ids = jnp.arange(per_peer, dtype=jnp.int32)

    def device_of(global_rows):
        return global_rows // col_count // q_local * ka_count + global_rows % col_count // row_count

    def prepare(table_flat):
        by_device = (
            table_flat.reshape(pb_count, q_local, ka_count, row_count)
            .transpose(0, 2, 1, 3)
            .reshape(dev_count, local_count)
        )
        mine = (device_of(by_device) == my_device).astype(jnp.int32)
        rank = jnp.cumsum(mine, 1) - 1
        source_local = (
            by_device // col_count % q_local * row_count + by_device % col_count % row_count
        )
        hits = mine[:, :, None] * (rank[:, :, None] == slot_ids[None, None, :]).astype(jnp.int32)
        send_index = jnp.sum(hits * source_local[:, :, None], 1).reshape(-1)
        return jnp.take(reducible, send_index, axis=1)

    def place(table_flat, received, column_map):
        source = table_flat[my_rows]
        source_dev = device_of(source)
        onehot = (source_dev[:, None] == jnp.arange(dev_count, dtype=jnp.int32)[None, :]).astype(
            jnp.int32
        )
        slot_index = jnp.sum((jnp.cumsum(onehot, 0) - onehot) * onehot, 1)
        picked = jnp.take(received, source_dev * per_peer + slot_index, axis=1)
        selector = (jnp.arange(col_count, dtype=jnp.int32)[:, None] == column_map[None, :]).astype(
            jnp.float32
        )
        picked = jnp.einsum("prk,km->prm", picked, selector, precision=lax.Precision.HIGHEST)
        return picked.reshape(2, q_local, row_count, col_count)

    table_a = row_maps[0].reshape(-1)
    table_b = row_maps[1].reshape(-1)
    send_a = prepare(table_a)
    send_b = prepare(table_b)
    recv_a, recv_b = in_one_piece((send_a, send_b), ("pb", "ka"), 1, 1, 0)
    crossed_a = vertex_cross_a + place(table_a, recv_a, col_maps[0])
    crossed_b = vertex_cross_b + place(table_b, recv_b, col_maps[1])
    return (ladder_out, crossed_a, crossed_b)


def solution(mesh):
    return jax.shard_map(
        per_device,
        mesh=mesh,
        in_specs=(
            P(None, "pb", "ka", None),
            P(None, "pb", "ka", None),
            P(None, "pb", "ka", None),
            P(None, "pb", None),
            P(),
            P(),
        ),
        out_specs=(P(None, "pb", "ka", None), P(None, "pb", "ka", None), P(None, "pb", "ka", None)),
        check_vma=False,
    )
```

profile of v0, /device:TPU:0, one launch (start us, length us, event | category | flops | bytes accessed | tf_op | source)
XLA Modules:
  0.0 306.2 jit_solution(12772516117283020420)
XLA Ops:
  7.2 2.1 copy.49
  9.4 1.3 copy.50
  13.1 4.7 %fusion.64 = (s32[4,32]{1,0:T(4,128)S(1)}, s32[4,32]{1,0:T(4,128)S(1)}) fusion(pred[4,32,4,32]{3,2,1,0:T(4,128)(4,1)S(1)} %eq.118, s32[]{:T(128)S(6)} %add.312, s32[4,4,32,32]{3,2,1,0:T(8,128)S(1)} %reshape_reshape_squeeze.7, pred[4,32,4,32]{3,2,1,0:T(4,128)(4,1)S(1)} %eq.113, s32[4,4,32,32]{3,2,1,0:T(8,128)S(1)} %reshape_reshape_squeeze.6), kind=kLoop, calls=%fused_computation.162 | loop fusion | flops 2162432 | bytes 164868 | tf_op jit(solution)/shard_map/reduce_sum | solution.py:88
  18.2 187.6 %all-gather.2.cloned.1.call-done = bf16[2,4,1024,1024]{3,2,0,1:T(8,128)(2,1)} async-done(((bf16[2,4,32,1024]{3,2,0,1:T(8,128)(2,1)}), bf16[2,4,1024,1024]{3,2,0,1:T(8,128)(2,1)}) %all-gather.2.cloned.1.call-update) | async-done | bytes 16777232 | tf_op jit(solution)/shard_map/all_gather | solution.py:45
  205.9 34.4 %while.10 = (s32[]{:T(128)}, f32[4,2,32,1024]{3,2,0,1:T(8,128)S(1)}, f32[4,2,32,1024]{3,2,1,0:T(8,128)S(1)}, f32[4,2,1024]{2,1,0:T(2,128)S(1)}, bf16[4,2,1024,10...) while((s32[]{:T(128)}, f32[4,2,32,1024]{3,2,0,1:T(8,128)S(1)}, f32[4,2,32,1024]{3,2,1,0:T(8,128)S(1)}, ...), condition=%wide.region_1.2_spmd, body=%wide.region_0.1_spmd.sunk | while | flops 1665269760 | bytes 49348760 | solution.py:51
  205.9 2.7 dynamic-slice_bitcast_fusion.5
  208.7 0.8 fusion.124
  209.6 0.8 fusion.126
  210.6 0.8 fusion.128
  211.6 0.8 fusion.130
  212.6 0.8 fusion.132
  213.6 0.8 fusion.134
  214.6 2.7 dynamic-slice_bitcast_fusion.5
  217.3 0.8 fusion.124
  218.2 0.8 fusion.126
  219.2 0.8 fusion.128
  220.2 0.8 fusion.130
  221.2 0.8 fusion.132
  222.2 0.8 fusion.134
  223.2 2.7 dynamic-slice_bitcast_fusion.5
  225.9 0.8 fusion.124
  226.8 0.8 fusion.126
  227.8 0.8 fusion.128
  228.8 0.8 fusion.130
  229.8 0.8 fusion.132
  230.8 0.8 fusion.134
  231.8 2.7 dynamic-slice_bitcast_fusion.5
  234.5 0.8 fusion.124
  235.4 0.8 fusion.126
  236.4 0.8 fusion.128
  237.4 0.8 fusion.130
  238.4 0.8 fusion.132
  239.3 0.8 fusion.134
  240.5 0.8 copy.26
  241.3 1.7 gather_fusion.3
  243.0 1.7 gather_fusion.2
  245.8 2.3 pad_maximum_fusion.7
  248.0 7.3 %all-to-all-start = ((f32[4,128,1024]{2,0,1:T(4,128)}), f32[4,128,1024]{2,0,1:T(4,128)S(1)}, u32[]{:S(2)}, u32[]{:S(2)}) async-start(f32[4,128,1024]{2,0,1:T(4,128)} %pad_maximum_fusion.7), calls=%async_computation | async-start | bytes 4194304 | tf_op jit(solution)/shard_map/all_to_all | solution.py:17
  255.4 1.1 gather_fusion
  256.8 1.1 gather_fusion.1
  258.7 26.1 %all-to-all-done = f32[4,128,1024]{2,0,1:T(4,128)S(1)} async-done(((f32[4,128,1024]{2,0,1:T(4,128)}), f32[4,128,1024]{2,0,1:T(4,128)S(1)}, u32[]{:S(2)}, u32[]{:S(2)}) %all-to-all-start) | async-done | bytes 2097184 | tf_op jit(solution)/shard_map/all_to_all | solution.py:17
  284.8 1.8 fusion.97
  286.6 3.0 gather_fusion.4
  290.2 2.3 fusion.45
  292.5 1.1 add.337
  293.6 1.7 gather_fusion.5
  295.8 2.3 fusion.48
  298.2 1.1 add.341
  (147 shorter events, 8.7 us)
Async XLA Ops:
  7.2 3.5 %copy-start.5 = (f32[2,4,1024]{2,1,0:T(4,128)S(1)}, f32[2,4,1024]{2,1,0:T(4,128)}, u32[]{:S(2)}) copy-start(f32[2,4,1024]{2,1,0:T(4,128)} %param.13) | copy-start | bytes 98308
  7.2 3.6 %copy-start.4 = (s32[2,16,1024]{2,1,0:T(8,128)S(1)}, s32[2,16,1024]{2,1,0:T(8,128)}, u32[]{:S(2)}) copy-start(s32[2,16,1024]{2,1,0:T(8,128)} %param.14) | copy-start | bytes 393220
  7.2 198.7 %all-gather.2.cloned.1.call-start = ((), (), s32[]{:S(2)}) async-start(), calls=%async_computation.1 | async-start | bytes 17301504 | tf_op jit(solution)/shard_map/all_gather | solution.py:45
  205.8 34.5 %copy-start = (f32[2,4,32,1024]{3,2,1,0:T(8,128)S(1)}, f32[2,4,32,1024]{3,2,1,0:T(8,128)}, u32[]{:S(2)}) copy-start(f32[2,4,32,1024]{3,2,1,0:T(8,128)} %param.10) | copy-start | bytes 3145732
  240.3 1.0 copy-start.3
  245.7 13.0 %copy-start.6 = (s32[2,1024]{1,0:T(2,128)S(1)}, s32[2,1024]{1,0:T(2,128)}, u32[]{:S(2)}) copy-start(s32[2,1024]{1,0:T(2,128)} %param.15) | copy-start | bytes 24580
  248.0 36.8 %all-to-all-start = ((f32[4,128,1024]{2,0,1:T(4,128)}), f32[4,128,1024]{2,0,1:T(4,128)S(1)}, u32[]{:S(2)}, u32[]{:S(2)}) async-start(f32[4,128,1024]{2,0,1:T(4,128)} %pad_maximum_fusion.7), calls=%async_computation | async-start | bytes 4194304 | tf_op jit(solution)/shard_map/all_to_all | solution.py:17
  286.6 5.9 %copy-start.1 = (f32[2,4,32,1024]{3,2,1,0:T(8,128)S(1)}, f32[2,4,32,1024]{3,2,1,0:T(8,128)}, u32[]{:S(2)}) copy-start(f32[2,4,32,1024]{3,2,1,0:T(8,128)} %param.11) | copy-start | bytes 3145732
  293.6 4.6 %copy-start.2 = (f32[2,4,32,1024]{3,2,1,0:T(8,128)S(1)}, f32[2,4,32,1024]{3,2,1,0:T(8,128)}, u32[]{:S(2)}) copy-start(f32[2,4,32,1024]{3,2,1,0:T(8,128)} %param.12) | copy-start | bytes 3145732
Sparse Core Ops, SparseCore 0:
  10.2 195.5 all-gather.1
where the time goes:
time: 306 us
  waiting for transfers between devices  214 us (70%)
  local copies, waits for them, and re-layouts  29.1 us (10%)
  matrix products  24.9 us (8%)
  other arithmetic  16 us (5%)
  between operations  14.5 us (5%)
  starting transfers between devices  7.32 us (2%)
    all_gather x1, waiting for transfers between devices, per_device(): whole_low = lax.all_gather(gamma_low, 'ka', axis=2, tiled=True)  188 us
    all_to_all x1, waiting for transfers between devices, in_one_piece(): lax.all_to_all(both, axis, split_axis=split_dim, concat_axis=concat_dim,...  26.1 us
    dot_general x24, matrix products, ladder_rows(): product = jnp.dot(left_op, right_op, preferred_element_type=jnp.float32)  20.3 us
    squeeze x4, local copies, waits for them, and re-layouts, ladder_rows(): right_op = jnp.concatenate([gathered[0], gathered[1]], 1)  10.8 us
    all_to_all x1, starting transfers between devices, in_one_piece(): lax.all_to_all(both, axis, split_axis=split_dim, concat_axis=concat_dim,...  7.28 us
  transfers between devices with their start and end apart: 2, of which 2 were waited for; matrix products, arithmetic and copies ran while one was open for 4% of the time, Pallas kernels for 0%

commit v1 on v0

--- a/solution.py
+++ b/solution.py
@@ -2,6 +2,7 @@
 import jax.numpy as jnp
 from jax import lax
 from jax.sharding import PartitionSpec as P
+from jax.lax import all_to_all, axis_size
 
 LADDER = 6
 
@@ -42,7 +43,9 @@
     row_count = vertex_ladder.shape[2]
     col_count = vertex_ladder.shape[3]
     gamma_low = vertex_ladder.astype(jnp.bfloat16)
-    whole_low = lax.all_gather(gamma_low, "ka", axis=2, tiled=True)
+    whole_low = jnp.concatenate(
+        all_to_all(jnp.stack(axis_size("ka") * [gamma_low], 0), "ka", 0, 0), 2
+    )
 
     def per_whole(loop_state, scan_items):
         vertex_rows, gathered, bubble_q = scan_items

time: 306 us -> 422 us (1.38)
  waiting for transfers between devices: 214 us -> 288 us
  starting transfers between devices: 7.32 us -> 41.7 us
  local copies, waits for them, and re-layouts: 29.1 us -> 47.5 us
  between operations: 14.5 us -> 1.12 us
    all_to_all x0 -> x1, waiting for transfers between devices: none -> 262 us  [per_device(): all_to_all(jnp.stack(axis_size('ka') * [gamma_low], 0), 'ka', 0, 0)]
    all_gather x1 -> x0, waiting for transfers between devices: 188 us -> none  [per_device(): whole_low = lax.all_gather(gamma_low, 'ka', axis=2, tiled=True)]
    all_to_all x1, starting transfers between devices: 7.28 us -> 32.7 us  [in_one_piece(): lax.all_to_all(both, axis, split_axis=split_dim, concat_axis=concat_dim,...]
    all_to_all x0 -> x1, local copies, waits for them, and re-layouts: none -> 14.2 us  [per_device(): all_to_all(jnp.stack(axis_size('ka') * [gamma_low], 0), 'ka', 0, 0)]
    dynamic_slice x0 -> x4, local copies, waits for them, and re-layouts: none -> 10.6 us  [per_device(): lax.scan(per_whole, jnp.int32(0), (jnp.moveaxis(vertex_ladder, 1, 0), jnp...]
    all_to_all x0 -> x1, starting transfers between devices: none -> 9.02 us  [per_device(): all_to_all(jnp.stack(axis_size('ka') * [gamma_low], 0), 'ka', 0, 0)]
    squeeze x4, local copies, waits for them, and re-layouts: 10.8 us -> 1.77 us  [ladder_rows(): right_op = jnp.concatenate([gathered[0], gathered[1]], 1)]
    another operation x0 -> x1, local copies, waits for them, and re-layouts: none -> 5.97 us  [per_device(): jnp.stack(axis_size('ka') * [gamma_low], 0)]
  transfers between devices with their start and end apart: 2 -> 2, of which waited for: 2 -> 2; matrix products, arithmetic and copies ran while one was open for 4% -> 3% of each run, Pallas kernels for 0% -> 0%
where the time goes in v1:
time: 422 us; the launch traced here: 421 us
  waiting for transfers between devices  288 us (68%)
  local copies, waits for them, and re-layouts  47.5 us (11%)
  starting transfers between devices  41.7 us (10%)
  matrix products  24.8 us (6%)
  other arithmetic  17.2 us (4%)
    all_to_all x1, waiting for transfers between devices, per_device(): all_to_all(jnp.stack(axis_size('ka') * [gamma_low], 0), 'ka', 0, 0)  262 us
    all_to_all x1, starting transfers between devices, in_one_piece(): lax.all_to_all(both, axis, split_axis=split_dim, concat_axis=concat_dim,...  32.7 us
    all_to_all x1, waiting for transfers between devices, in_one_piece(): lax.all_to_all(both, axis, split_axis=split_dim, concat_axis=concat_dim,...  26.3 us
    dot_general x24, matrix products, ladder_rows(): product = jnp.dot(left_op, right_op, preferred_element_type=jnp.float32)  20.2 us
    all_to_all x1, local copies, waits for them, and re-layouts, per_device(): all_to_all(jnp.stack(axis_size('ka') * [gamma_low], 0), 'ka', 0, 0)  14.2 us
    dynamic_slice x4, local copies, waits for them, and re-layouts, per_device(): lax.scan(per_whole, jnp.int32(0), (jnp.moveaxis(vertex_ladder, 1, 0), jnp...  10.6 us
    all_to_all x1, starting transfers between devices, per_device(): all_to_all(jnp.stack(axis_size('ka') * [gamma_low], 0), 'ka', 0, 0)  9.02 us
  transfers between devices with their start and end apart: 2, of which 2 were waited for; matrix products, arithmetic and copies ran while one was open for 3% of the time, Pallas kernels for 0%

profile of v1, /device:TPU:0, one launch (start us, length us, event | category | flops | bytes accessed | tf_op | source)
XLA Modules:
  0.0 421.4 jit_solution(66641973159477867)
XLA Ops:
  0.6 1.3 convert_element_type.35
  2.0 6.0 %stack.38 = bf16[32,2,4,32,1024]{4,3,1,2,0:T(8,128)(2,1)} broadcast(bf16[2,4,32,1024]{3,2,0,1:T(8,128)(2,1)S(1)} %copy.47), dimensions={1,2,3,4} | broadcast | bytes 17301504 | tf_op jit(solution)/shard_map/stack | solution.py:47
  8.0 9.0 %all-to-all-start = ((bf16[32,2,4,32,1024]{4,3,1,2,0:T(8,128)(2,1)}), bf16[32,2,4,32,1024]{4,3,1,2,0:T(8,128)(2,1)}, u32[]{:S(2)}, u32[]{:S(2)}) async-start(bf16[32,2,4,32,1024]{4,3,1,2,0:T(8,128)(2,1)} %stack.38), calls=%async_computation | async-start | bytes 33554432 | tf_op jit(solution)/shard_map/all_to_all | solution.py:47
  19.5 4.7 %fusion.64 = (s32[4,32]{1,0:T(4,128)S(1)}, s32[4,32]{1,0:T(4,128)S(1)}) fusion(pred[4,32,4,32]{3,2,1,0:T(4,128)(4,1)S(1)} %eq.118, s32[]{:T(128)S(6)} %add.312, s32[4,4,32,32]{3,2,1,0:T(8,128)S(1)} %reshape_reshape_squeeze.7, pred[4,32,4,32]{3,2,1,0:T(4,128)(4,1)S(1)} %eq.113, s32[4,4,32,32]{3,2,1,0:T(8,128)S(1)} %reshape_reshape_squeeze.6), kind=kLoop, calls=%fused_computation.162 | loop fusion | flops 2162432 | bytes 164868 | tf_op jit(solution)/shard_map/reduce_sum | solution.py:91
  24.6 261.8 %all-to-all-done = bf16[32,2,4,32,1024]{4,3,1,2,0:T(8,128)(2,1)} async-done(((bf16[32,2,4,32,1024]{4,3,1,2,0:T(8,128)(2,1)}), bf16[32,2,4,32,1024]{4,3,1,2,0:T(8,128)(2,1)}, u32[]{:S(2)}, u32[]{:S(2)}) %all-to-all-start) | async-done | bytes 16777248 | tf_op jit(solution)/shard_map/all_to_all | solution.py:47
  286.5 14.2 %copy.48 = bf16[32,2,4,32,1024]{4,3,0,2,1:T(8,128)(2,1)} copy(bf16[32,2,4,32,1024]{4,3,1,2,0:T(8,128)(2,1)} %all-to-all-done) | data formatting | bytes 33554432 | tf_op jit(solution)/shard_map/all_to_all | solution.py:47
  300.6 36.1 %while.10 = (s32[]{:T(128)}, f32[4,2,32,1024]{3,2,0,1:T(8,128)S(1)}, f32[4,2,32,1024]{3,2,1,0:T(8,128)S(1)}, f32[4,2,1024]{2,1,0:T(2,128)S(1)}, bf16[4,2,1024,10...) while((s32[]{:T(128)}, f32[4,2,32,1024]{3,2,0,1:T(8,128)S(1)}, f32[4,2,32,1024]{3,2,1,0:T(8,128)S(1)}, ...), condition=%wide.region_1.2_spmd, body=%wide.region_0.1_spmd.sunk | while | flops 1665269760 | bytes 57737356 | solution.py:54
  300.7 2.6 dynamic-slice_bitcast_fusion.4
  303.8 0.8 fusion.124
  304.8 0.8 fusion.126
  305.7 0.8 fusion.128
  306.7 0.8 fusion.130
  307.7 0.8 fusion.132
  308.7 0.8 fusion.134
  309.7 2.6 dynamic-slice_bitcast_fusion.4
  312.8 0.8 fusion.124
  313.8 0.8 fusion.126
  314.7 0.8 fusion.128
  315.7 0.8 fusion.130
  316.7 0.8 fusion.132
  317.6 0.8 fusion.134
  318.7 2.6 dynamic-slice_bitcast_fusion.4
  321.8 0.8 fusion.124
  322.7 0.8 fusion.126
  323.7 0.8 fusion.128
  324.7 0.8 fusion.130
  325.7 0.8 fusion.132
  326.6 0.8 fusion.134
  327.7 2.6 dynamic-slice_bitcast_fusion.4
  330.7 0.8 fusion.124
  331.7 0.8 fusion.126
  332.7 0.8 fusion.128
  334.6 0.8 fusion.132
  335.6 0.8 fusion.134
  337.7 1.7 gather_fusion.2
  339.4 1.7 gather_fusion.3
  342.2 2.3 pad_maximum_fusion.7
  344.5 32.7 %all-to-all-start.1 = ((f32[4,128,1024]{2,0,1:T(4,128)}), f32[4,128,1024]{2,0,1:T(4,128)S(1)}, u32[]{:S(2)}, u32[]{:S(2)}) async-start(f32[4,128,1024]{2,0,1:T(4,128)} %pad_maximum_fusion.7), calls=%async_computation.1 | async-start | bytes 4194304 | tf_op jit(solution)/shard_map/all_to_all | solution.py:18
  377.2 1.1 gather_fusion.1
  378.7 1.1 gather_fusion
  380.6 26.3 %all-to-all-done.1 = f32[4,128,1024]{2,0,1:T(4,128)S(1)} async-done(((f32[4,128,1024]{2,0,1:T(4,128)}), f32[4,128,1024]{2,0,1:T(4,128)S(1)}, u32[]{:S(2)}, u32[]{:S(2)}) %all-to-all-start.1) | async-done | bytes 2097184 | tf_op jit(solution)/shard_map/all_to_all | solution.py:18
  406.9 1.8 fusion.97
  408.7 3.0 gather_fusion.5
  412.2 2.3 fusion.48
  414.6 1.1 add.341
  415.7 1.7 gather_fusion.4
  417.9 2.3 fusion.45
  420.3 1.1 add.337
  (155 shorter events, 12.2 us)
Async XLA Ops:
  8.0 9.0 %copy-start = (f32[2,4,32,1024]{3,2,1,0:T(8,128)S(1)}, f32[2,4,32,1024]{3,2,1,0:T(8,128)}, u32[]{:S(2)}) copy-start(f32[2,4,32,1024]{3,2,1,0:T(8,128)} %param.10) | copy-start | bytes 3145732
  8.0 9.2 %copy-start.5 = (s32[2,16,1024]{2,1,0:T(8,128)S(1)}, s32[2,16,1024]{2,1,0:T(8,128)}, u32[]{:S(2)}) copy-start(s32[2,16,1024]{2,1,0:T(8,128)} %param.14) | copy-start | bytes 393220
  8.0 278.5 %all-to-all-start = ((bf16[32,2,4,32,1024]{4,3,1,2,0:T(8,128)(2,1)}), bf16[32,2,4,32,1024]{4,3,1,2,0:T(8,128)(2,1)}, u32[]{:S(2)}, u32[]{:S(2)}) async-start(bf16[32,2,4,32,1024]{4,3,1,2,0:T(8,128)(2,1)} %stack.38), calls=%async_computation | async-start | bytes 33554432 | tf_op jit(solution)/shard_map/all_to_all | solution.py:47
  17.0 7.3 %copy-start.6 = (f32[2,4,1024]{2,1,0:T(4,128)S(1)}, f32[2,4,1024]{2,1,0:T(4,128)}, u32[]{:S(2)}) copy-start(f32[2,4,1024]{2,1,0:T(4,128)} %param.13) | copy-start | bytes 98308
  24.6 276.0 %copy-start.3 = (f32[4,2,32,1024]{3,2,0,1:T(8,128)S(1)}, f32[4,2,32,1024]{3,2,0,1:T(8,128)}, u32[]{:S(2)}) copy-start(f32[4,2,32,1024]{3,2,0,1:T(8,128)} %custom-call.12) | copy-start | bytes 3145732
  336.7 1.0 copy-start.4
  342.2 38.4 %copy-start.7 = (s32[2,1024]{1,0:T(2,128)S(1)}, s32[2,1024]{1,0:T(2,128)}, u32[]{:S(2)}) copy-start(s32[2,1024]{1,0:T(2,128)} %param.15) | copy-start | bytes 24580
  344.5 62.4 %all-to-all-start.1 = ((f32[4,128,1024]{2,0,1:T(4,128)}), f32[4,128,1024]{2,0,1:T(4,128)S(1)}, u32[]{:S(2)}, u32[]{:S(2)}) async-start(f32[4,128,1024]{2,0,1:T(4,128)} %pad_maximum_fusion.7), calls=%async_computation.1 | async-start | bytes 4194304 | tf_op jit(solution)/shard_map/all_to_all | solution.py:18
  408.7 5.9 %copy-start.1 = (f32[2,4,32,1024]{3,2,1,0:T(8,128)S(1)}, f32[2,4,32,1024]{3,2,1,0:T(8,128)}, u32[]{:S(2)}) copy-start(f32[2,4,32,1024]{3,2,1,0:T(8,128)} %param.12) | copy-start | bytes 3145732
  415.7 4.6 %copy-start.2 = (f32[2,4,32,1024]{3,2,1,0:T(8,128)S(1)}, f32[2,4,32,1024]{3,2,1,0:T(8,128)}, u32[]{:S(2)}) copy-start(f32[2,4,32,1024]{3,2,1,0:T(8,128)} %param.11) | copy-start | bytes 3145732
